TPU v7x, 256 devices: a whole 4x4x8 slice. The times are simulated.
256 devices in a mesh: seq: 16 (over y, x), dp: 16 (over z, core).
Axes of the slice: x: 4, y: 4, z: 8, core: 2. Of those that a mesh axis runs over, the one named last changes fastest.
Arguments:
- queries: bfloat16 [128, 256, 4096], P(None, ('seq', 'dp')), may hold values from -8 to 8
- keys_in: bfloat16 [128, 256, 4096], P(None, ('seq', 'dp')), may hold values from -8 to 8
- values: bfloat16 [128, 256, 4096], P(None, ('seq', 'dp')), may hold values from -6 to 6
- grad_out: bfloat16 [10, 4096, 4096], P(None, ('seq', 'dp')), may hold values from -6 to 6
- doc_lengths: int32 [24], replicated, may hold values from 1 to 2560, as said below
- doc_group: int32 [24], replicated, may hold values from 0 to 15, as said below
Outputs:
- attended: bfloat16 [10, 4096, 4096], P(None, ('seq', 'dp'))
- grad_queries: bfloat16 [128, 256, 4096], P(None, ('seq', 'dp'))
- grad_keys: bfloat16 [128, 256, 4096], P(None, ('seq', 'dp'))
- grad_values: bfloat16 [128, 256, 4096], P(None, ('seq', 'dp'))
Inputs may be any that keep to these rules, and one draw needn't show every extreme that they name: `doc_lengths`: the documents lie one after another in the packed batch in index order and their lengths sum to 32768. The documents of one group are consecutive, groups in increasing order; every group holds a whole multiple of 256 tokens, at most 2560, and some group holds exactly that many. `doc_group`: never falls from one document to the next; every group takes at least one document.
All inputs are finite; a program needn't handle non-finite values.
Results may differ from a plain program's by a relative error of at most 0.02.
Values may be sent and summed in bfloat16 or wider, within the bound.
A program may use at most 64 MiB of HBM per device.

v0:
```python
import jax
import jax.numpy as jnp
import numpy as np
from jax import lax
from jax.sharding import PartitionSpec as P

HEAD = 128
NEGATIVE_FILL = -1e30


def group_tables(doc_lengths, doc_group, group_count, per_unit):
    doc_ends = jnp.cumsum(doc_lengths)
    member = (doc_group[:, None] == jnp.arange(group_count, dtype=jnp.int32)[None, :]).astype(
        jnp.int32
    )
    group_units = jnp.sum(member * doc_lengths[:, None], axis=0) // per_unit
    first_unit = jnp.cumsum(group_units) - group_units
    return (doc_ends, group_units, first_unit)


def attend_group(
    head_q, head_k, head_v, head_do, token_ids, doc_query, doc_key, row_live, block_rows
):
    row_count, head_count, head_dim = head_q.shape
    blocks = row_count // block_rows
    score_scale = head_dim ** (-0.5)
    later, earlier = np.tril_indices(blocks)
    query_block = jnp.asarray(later, dtype=jnp.int32)
    key_block = jnp.asarray(earlier, dtype=jnp.int32)
    pair_total = int(later.shape[0])
    block_docs = doc_query.reshape(blocks, block_rows)
    live_blocks = row_live.reshape(blocks, block_rows)
    lowest = jnp.min(jnp.where(live_blocks, block_docs, 1 << 30), axis=1)
    highest = jnp.max(jnp.where(live_blocks, block_docs, -1), axis=1)
    needed = (
        (highest[key_block] >= lowest[query_block])
        & (lowest[key_block] <= highest[key_block])
        & (lowest[query_block] <= highest[query_block])
    )

    def tile_scores(pair_index):
        q_start = query_block[pair_index] * block_rows
        k_start = key_block[pair_index] * block_rows
        q_rows = lax.dynamic_slice_in_dim(head_q, q_start, block_rows, 0)
        k_rows = lax.dynamic_slice_in_dim(head_k, k_start, block_rows, 0)
        same_doc = (
            lax.dynamic_slice_in_dim(doc_query, q_start, block_rows, 0)[:, None]
            == lax.dynamic_slice_in_dim(doc_key, k_start, block_rows, 0)[None, :]
        )
        earlier_key = (
            lax.dynamic_slice_in_dim(token_ids, k_start, block_rows, 0)[None, :]
            <= lax.dynamic_slice_in_dim(token_ids, q_start, block_rows, 0)[:, None]
        )
        scores = (
            jnp.einsum("qhe,khe->qhk", q_rows, k_rows, preferred_element_type=jnp.float32)
            * score_scale
        )
        return (q_start, k_start, q_rows, k_rows, scores, (same_doc & earlier_key)[:, None, :])

    def stats_step(pair_index, loop_state):

        def stats_compute(inner_state):
            row_top, row_total = inner_state
            q_start, k_start, q_rows, k_rows, scores, allowed = tile_scores(pair_index)
            old_top = lax.dynamic_slice_in_dim(row_top, q_start, block_rows, 0)
            old_total = lax.dynamic_slice_in_dim(row_total, q_start, block_rows, 0)
            new_top = jnp.maximum(
                old_top, jnp.max(jnp.where(allowed, scores, NEGATIVE_FILL), axis=2)
            )
            exp_terms = jnp.sum(
                jnp.where(allowed, jnp.exp(scores - new_top[:, :, None]), 0.0), axis=2
            )
            new_total = old_total * jnp.exp(old_top - new_top) + exp_terms
            return (
                lax.dynamic_update_slice_in_dim(row_top, new_top, q_start, 0),
                lax.dynamic_update_slice_in_dim(row_total, new_total, q_start, 0),
            )

        return lax.cond(needed[pair_index], stats_compute, lambda unchanged: unchanged, loop_state)

    start_state = (
        jnp.full((row_count, head_count), NEGATIVE_FILL, jnp.float32),
        jnp.zeros((row_count, head_count), jnp.float32),
    )
    row_top, row_total = lax.fori_loop(0, pair_total, stats_step, start_state)
    log_total = jnp.where(row_live[:, None], row_top + jnp.log(row_total), 0.0)

    def value_step(pair_index, accumulated):

        def value_compute(inner_state):
            q_start, k_start, q_rows, k_rows, scores, allowed = tile_scores(pair_index)
            row_log = lax.dynamic_slice_in_dim(log_total, q_start, block_rows, 0)
            weight = jnp.where(allowed, jnp.exp(scores - row_log[:, :, None]), 0.0).astype(
                jnp.bfloat16
            )
            v_rows = lax.dynamic_slice_in_dim(head_v, k_start, block_rows, 0)
            part_sum = jnp.einsum(
                "qhk,khe->qhe", weight, v_rows, preferred_element_type=jnp.float32
            )
            current = lax.dynamic_slice_in_dim(inner_state, q_start, block_rows, 0)
            return lax.dynamic_update_slice_in_dim(inner_state, current + part_sum, q_start, 0)

        return lax.cond(needed[pair_index], value_compute, lambda unchanged: unchanged, accumulated)

    accumulated = lax.fori_loop(
        0, pair_total, value_step, jnp.zeros((row_count, head_count, head_dim), jnp.float32)
    )
    attended = accumulated.astype(jnp.bfloat16)
    delta_all = jnp.sum(head_do.astype(jnp.float32) * attended.astype(jnp.float32), axis=2)

    def grad_step(pair_index, loop_state):

        def grad_compute(inner_state):
            grad_q, grad_k, grad_v = inner_state
            q_start, k_start, q_rows, k_rows, scores, allowed = tile_scores(pair_index)
            row_log = lax.dynamic_slice_in_dim(log_total, q_start, block_rows, 0)
            row_delta = lax.dynamic_slice_in_dim(delta_all, q_start, block_rows, 0)
            weight_full = jnp.where(allowed, jnp.exp(scores - row_log[:, :, None]), 0.0)
            do_rows = lax.dynamic_slice_in_dim(head_do, q_start, block_rows, 0)
            v_rows = lax.dynamic_slice_in_dim(head_v, k_start, block_rows, 0)
            grad_prob = jnp.einsum(
                "qhe,khe->qhk", do_rows, v_rows, preferred_element_type=jnp.float32
            )
            grad_score = (weight_full * (grad_prob - row_delta[:, :, None])).astype(jnp.bfloat16)
            add_values = jnp.einsum(
                "qhk,qhe->khe",
                weight_full.astype(jnp.bfloat16),
                do_rows,
                preferred_element_type=jnp.float32,
            )
            add_queries = jnp.einsum(
                "qhk,khe->qhe", grad_score, k_rows, preferred_element_type=jnp.float32
            )
            add_keys = jnp.einsum(
                "qhk,qhe->khe", grad_score, q_rows, preferred_element_type=jnp.float32
            )
            grad_q = lax.dynamic_update_slice_in_dim(
                grad_q,
                lax.dynamic_slice_in_dim(grad_q, q_start, block_rows, 0) + add_queries,
                q_start,
                0,
            )
            grad_k = lax.dynamic_update_slice_in_dim(
                grad_k,
                lax.dynamic_slice_in_dim(grad_k, k_start, block_rows, 0) + add_keys,
                k_start,
                0,
            )
            grad_v = lax.dynamic_update_slice_in_dim(
                grad_v,
                lax.dynamic_slice_in_dim(grad_v, k_start, block_rows, 0) + add_values,
                k_start,
                0,
            )
            return (grad_q, grad_k, grad_v)

        return lax.cond(needed[pair_index], grad_compute, lambda unchanged: unchanged, loop_state)

    zero_grads = jnp.zeros((row_count, head_count, head_dim), jnp.float32)
    grad_q, grad_k, grad_v = lax.fori_loop(
        0, pair_total, grad_step, (zero_grads, zero_grads, zero_grads)
    )
    return (
        attended,
        (grad_q * score_scale).astype(jnp.bfloat16),
        (grad_k * score_scale).astype(jnp.bfloat16),
        grad_v.astype(jnp.bfloat16),
    )


def to_groups(first_part, second_part, third_part):
    return (
        lax.all_to_all(first_part, "dp", split_axis=1, concat_axis=1, tiled=True),
        lax.all_to_all(second_part, "dp", split_axis=1, concat_axis=1, tiled=True),
        lax.all_to_all(third_part, "dp", split_axis=1, concat_axis=1, tiled=True),
    )


def to_heads(first_part, second_part, third_part, fourth_part):
    return (
        lax.all_to_all(first_part, "seq", split_axis=2, concat_axis=1, tiled=True),
        lax.all_to_all(second_part, "seq", split_axis=2, concat_axis=1, tiled=True),
        lax.all_to_all(third_part, "seq", split_axis=2, concat_axis=1, tiled=True),
        lax.all_to_all(fourth_part, "seq", split_axis=2, concat_axis=1, tiled=True),
    )


def from_heads(first_part, second_part, third_part, fourth_part):
    return (
        lax.all_to_all(first_part, "seq", split_axis=1, concat_axis=2, tiled=True),
        lax.all_to_all(second_part, "seq", split_axis=1, concat_axis=2, tiled=True),
        lax.all_to_all(third_part, "seq", split_axis=1, concat_axis=2, tiled=True),
        lax.all_to_all(fourth_part, "seq", split_axis=1, concat_axis=2, tiled=True),
    )


def to_packed(first_part, second_part, third_part):
    return (
        lax.all_to_all(first_part, "dp", split_axis=1, concat_axis=1, tiled=True),
        lax.all_to_all(second_part, "dp", split_axis=1, concat_axis=1, tiled=True),
        lax.all_to_all(third_part, "dp", split_axis=1, concat_axis=1, tiled=True),
    )


def body(queries, keys_in, values, grad_out, doc_lengths, doc_group):
    seq_count = lax.axis_size("seq")
    group_count = lax.axis_size("dp")
    devices = seq_count * group_count
    local_rows = queries.shape[0]
    features = queries.shape[2]
    head_dim = HEAD
    local_heads = features // (seq_count * head_dim)
    capacity = grad_out.shape[0]
    doc_ends, group_units, first_unit = group_tables(doc_lengths, doc_group, group_count, devices)
    slot_ids = jnp.arange(capacity, dtype=jnp.int32)[:, None]
    filled = slot_ids < group_units[None, :]
    source_row = jnp.where(filled, first_unit[None, :] + slot_ids, 0).reshape(-1)
    row_ids = jnp.arange(local_rows, dtype=jnp.int32)
    row_group = jnp.sum((first_unit + group_units)[None, :] <= row_ids[:, None], axis=1)
    row_first = jnp.sum(
        jnp.where(
            jnp.arange(group_count, dtype=jnp.int32)[None, :] == row_group[:, None],
            first_unit[None, :],
            0,
        ),
        axis=1,
    )
    target_row = (row_ids - row_first) * group_count + row_group

    def pack_rows(local):
        taken_rows = jnp.take(local, source_row, axis=0).reshape(
            (capacity, group_count) + local.shape[1:]
        )
        keep_mask = filled.reshape((capacity, group_count) + (1,) * (local.ndim - 1))
        return jnp.where(keep_mask, taken_rows, jnp.zeros((), local.dtype))

    def unpack_rows(balanced):
        flat_rows = balanced.reshape((capacity * group_count,) + balanced.shape[2:])
        return jnp.take(flat_rows, target_row, axis=0)

    head_shape = (seq_count, local_heads, head_dim)
    group_rows = capacity * group_count * seq_count
    flat_q = queries.reshape(local_rows, features)
    flat_k = keys_in.reshape(local_rows, features)
    flat_v = values.reshape(local_rows, features)
    cot_rows = grad_out.reshape((capacity * group_count, 1) + head_shape)
    moved_q, moved_k, moved_v = to_groups(pack_rows(flat_q), pack_rows(flat_k), pack_rows(flat_v))
    lead_shape = (capacity * group_count, 1) + head_shape
    head_q, head_k, head_v, head_do = to_heads(
        moved_q.reshape(lead_shape),
        moved_k.reshape(lead_shape),
        moved_v.reshape(lead_shape),
        cot_rows,
    )
    work_shape = (group_rows, local_heads, head_dim)
    head_q = head_q.reshape(work_shape)
    head_k = head_k.reshape(work_shape)
    head_v = head_v.reshape(work_shape)
    head_do = head_do.reshape(work_shape)
    group_index = lax.axis_index("dp")
    slot_axis = jnp.arange(capacity, dtype=jnp.int32)[:, None, None]
    data_axis = jnp.arange(group_count, dtype=jnp.int32)[None, :, None]
    seq_axis = jnp.arange(seq_count, dtype=jnp.int32)[None, None, :]
    token_ids = (
        (first_unit[group_index] + slot_axis) * devices + seq_axis * group_count + data_axis
    ).reshape(-1)
    row_live = jnp.broadcast_to(
        slot_axis < group_units[group_index], (capacity, group_count, seq_count)
    ).reshape(-1)
    doc_of = jnp.sum(doc_ends[None, :] <= token_ids[:, None], axis=1)
    doc_query = jnp.where(row_live, doc_of, -1)
    doc_key = jnp.where(row_live, doc_of, -2)
    divisors = [
        factor
        for factor in range(1, capacity + 1)
        if capacity % factor == 0 and factor * devices <= 512
    ]
    block_rows = divisors[-1] * devices
    attended, grad_q, grad_k, grad_v = attend_group(
        head_q, head_k, head_v, head_do, token_ids, doc_query, doc_key, row_live, block_rows
    )
    back_shape = (capacity * group_count, seq_count, 1, local_heads, head_dim)
    seq_out, seq_q, seq_k, seq_v = from_heads(
        attended.reshape(back_shape),
        grad_q.reshape(back_shape),
        grad_k.reshape(back_shape),
        grad_v.reshape(back_shape),
    )
    flat_shape = (capacity, group_count, features)
    home_q, home_k, home_v = to_packed(
        seq_q.reshape(flat_shape), seq_k.reshape(flat_shape), seq_v.reshape(flat_shape)
    )
    out_q = unpack_rows(home_q)
    out_k = unpack_rows(home_k)
    out_v = unpack_rows(home_v)
    packed_shape = (local_rows, 1, features)
    return (
        seq_out.reshape(capacity, group_count, features),
        out_q.reshape(packed_shape),
        out_k.reshape(packed_shape),
        out_v.reshape(packed_shape),
    )


def solution(mesh):
    return jax.shard_map(
        body,
        mesh=mesh,
        in_specs=(
            P(None, ("seq", "dp"), None),
            P(None, ("seq", "dp"), None),
            P(None, ("seq", "dp"), None),
            P(None, ("seq", "dp"), None),
            P(),
            P(),
        ),
        out_specs=(
            P(None, ("seq", "dp"), None),
            P(None, ("seq", "dp"), None),
            P(None, ("seq", "dp"), None),
            P(None, ("seq", "dp"), None),
        ),
        check_vma=False,
    )
```

profile of v0, /device:TPU:1, one launch (start us, length us, event | category | flops | bytes accessed | tf_op | source)
XLA Modules:
  0.0 1028.3 jit_solution(3317540687620245920)
XLA Ops:
  5.9 7.7 all-to-all-start.7
  25.8 10.6 %copy_select_fusion = (bf16[10,16,4096]{2,0,1:T(8,128)(2,1)S(1)}, bf16[10,16,4096]{2,0,1:T(8,128)(2,1)}, bf16[10,16,4096]{2,0,1:T(8,128)(2,1)}) fusion(bf16[10,16,4096]{2,1,0:T(8,128)(2,1)} %bitcast.152, pred[10,16]{0,1:T(8,128)(4,1)S(1)} %copy.155, bf16[10,16,4096]{2,1,0:T(8,128)(2,1)} %bitcast.153, bf16[10,16,4096]{2,1,0:T(8,128)(2,1)} %bitcast.154), kind=kLoop, calls=%fused_computation.84 | loop fusion | flops 1966080 | bytes 7864480 | tf_op jit(solution)/shard_map/jit(_where)/select_n | solution.py:235
  36.4 60.6 %all_to_all.102 = bf16[10,16,4096]{2,0,1:T(8,128)(2,1)} all-to-all(bf16[10,16,4096]{2,0,1:T(8,128)(2,1)} %get-tuple-element.1227), channel_id=1, replica_groups=mesh['seq'=16,'dp'=16] {'dp'}, dimensions={1} | all-to-all | bytes 2621440 | tf_op jit(solution)/shard_map/all_to_all | solution.py:174
  97.0 53.7 %all_to_all.103 = bf16[10,16,4096]{2,0,1:T(8,128)(2,1)} all-to-all(bf16[10,16,4096]{2,0,1:T(8,128)(2,1)S(1)} %get-tuple-element.1226), channel_id=1, replica_groups=mesh['seq'=16,'dp'=16] {'dp'}, dimensions={1} | all-to-all | bytes 2621440 | tf_op jit(solution)/shard_map/all_to_all | solution.py:173
  165.1 37.7 %all-to-all-done = bf16[10,16,4096]{2,0,1:T(8,128)(2,1)S(1)} async-done(((bf16[10,16,4096]{2,0,1:T(8,128)(2,1)}), bf16[10,16,4096]{2,0,1:T(8,128)(2,1)S(1)}, u32[]{:S(2)}, u32[]{:S(2)}) %all-to-all-start) | async-done | bytes 1310752 | tf_op jit(solution)/shard_map/all_to_all | solution.py:175
  220.4 9.8 all-to-all-done.3
  243.5 9.0 all-to-all-done.5
  269.4 117.6 %while.54 = (s32[]{:T(128)}, f32[2560,2]{0,1:T(2,128)S(1)}, f32[2560,2]{0,1:T(2,128)S(1)}, pred[15]{0:T(512)(128)(4,1)S(1)}, s32[2560]{0:T(1024)S(1)}, /*index=5...) while((s32[]{:T(128)}, f32[2560,2]{0,1:T(2,128)S(1)}, ...), condition=%wide.region_13.15_spmd.clone.clone, body=%wide.region_8.14_spmd.sunk.clone.clone.sunk | while | flops 138678800 | bytes 5712918 | solution.py:85
  393.6 130.8 %while.55 = (s32[]{:T(128)}, f32[2560,2,128]{0,2,1:T(8,128)}, pred[15]{0:T(512)(128)(4,1)S(1)}, bf16[2560,2,128]{0,2,1:T(8,128)(2,1)}, s32[2560]{0:T(1024)S(1)},...) while((s32[]{:T(128)}, f32[2560,2,128]{0,2,1:T(8,128)}, ...), condition=%wide.region_17.19_spmd.clone.clone, body=%wide.region_14.18_spmd.sunk.clone.clone.sunk | while | flops 271452672 | bytes 2450426 | solution.py:105
  531.5 229.7 %while.56 = (s32[]{:T(128)}, f32[2560,2,128]{0,2,1:T(8,128)}, f32[2560,2,128]{0,2,1:T(8,128)}, f32[2560,2,128]{0,2,1:T(8,128)S(1)}, pred[15]{0:T(512)(128)(4,1)S...) while((s32[]{:T(128)}, f32[2560,2,128]{0,2,1:T(8,128)}, ...), condition=%wide.region_22.24_spmd.clone.clone, body=%wide.region_19.23_spmd.sunk.clone.clone.sunk | while | flops 675940864 | bytes 15043730 | solution.py:160
  533.1 14.0 %conditional.17 = ((f32[2560,2,128]{0,2,1:T(8,128)}, f32[2560,2,128]{0,2,1:T(8,128)}, f32[2560,2,128]{0,2,1:T(8,128)S(1)})) conditional(s32[]{:T(128)} %bitcast.135, (f32[2560,2,128]{0,2,1:T(8,128)}, f32[2560,2,128]{0,2,1:T(8,128)}, f32[2560,2,128]{0,2,1:T(8,128)S(1)}) %tuple.202, (s32[]{:T(128)}, f32[2560,2,128]{0,2,1:T(8,128)}, ...), branch_computations={%region_20.21_spmd, %region_21.22_spmd.clone} | conditional | flops 675940864 | bytes 15033202 | solution.py:157
  548.4 14.1 %conditional.17 = ((f32[2560,2,128]{0,2,1:T(8,128)}, f32[2560,2,128]{0,2,1:T(8,128)}, f32[2560,2,128]{0,2,1:T(8,128)S(1)})) conditional(s32[]{:T(128)} %bitcast.135, (f32[2560,2,128]{0,2,1:T(8,128)}, f32[2560,2,128]{0,2,1:T(8,128)}, f32[2560,2,128]{0,2,1:T(8,128)S(1)}) %tuple.202, (s32[]{:T(128)}, f32[2560,2,128]{0,2,1:T(8,128)}, ...), branch_computations={%region_20.21_spmd, %region_21.22_spmd.clone} | conditional | flops 675940864 | bytes 15033202 | solution.py:157
  563.7 14.0 %conditional.17 = ((f32[2560,2,128]{0,2,1:T(8,128)}, f32[2560,2,128]{0,2,1:T(8,128)}, f32[2560,2,128]{0,2,1:T(8,128)S(1)})) conditional(s32[]{:T(128)} %bitcast.135, (f32[2560,2,128]{0,2,1:T(8,128)}, f32[2560,2,128]{0,2,1:T(8,128)}, f32[2560,2,128]{0,2,1:T(8,128)S(1)}) %tuple.202, (s32[]{:T(128)}, f32[2560,2,128]{0,2,1:T(8,128)}, ...), branch_computations={%region_20.21_spmd, %region_21.22_spmd.clone} | conditional | flops 675940864 | bytes 15033202 | solution.py:157
  579.0 14.0 %conditional.17 = ((f32[2560,2,128]{0,2,1:T(8,128)}, f32[2560,2,128]{0,2,1:T(8,128)}, f32[2560,2,128]{0,2,1:T(8,128)S(1)})) conditional(s32[]{:T(128)} %bitcast.135, (f32[2560,2,128]{0,2,1:T(8,128)}, f32[2560,2,128]{0,2,1:T(8,128)}, f32[2560,2,128]{0,2,1:T(8,128)S(1)}) %tuple.202, (s32[]{:T(128)}, f32[2560,2,128]{0,2,1:T(8,128)}, ...), branch_computations={%region_20.21_spmd, %region_21.22_spmd.clone} | conditional | flops 675940864 | bytes 15033202 | solution.py:157
  594.3 14.0 %conditional.17 = ((f32[2560,2,128]{0,2,1:T(8,128)}, f32[2560,2,128]{0,2,1:T(8,128)}, f32[2560,2,128]{0,2,1:T(8,128)S(1)})) conditional(s32[]{:T(128)} %bitcast.135, (f32[2560,2,128]{0,2,1:T(8,128)}, f32[2560,2,128]{0,2,1:T(8,128)}, f32[2560,2,128]{0,2,1:T(8,128)S(1)}) %tuple.202, (s32[]{:T(128)}, f32[2560,2,128]{0,2,1:T(8,128)}, ...), branch_computations={%region_20.21_spmd, %region_21.22_spmd.clone} | conditional | flops 675940864 | bytes 15033202 | solution.py:157
  609.6 14.0 %conditional.17 = ((f32[2560,2,128]{0,2,1:T(8,128)}, f32[2560,2,128]{0,2,1:T(8,128)}, f32[2560,2,128]{0,2,1:T(8,128)S(1)})) conditional(s32[]{:T(128)} %bitcast.135, (f32[2560,2,128]{0,2,1:T(8,128)}, f32[2560,2,128]{0,2,1:T(8,128)}, f32[2560,2,128]{0,2,1:T(8,128)S(1)}) %tuple.202, (s32[]{:T(128)}, f32[2560,2,128]{0,2,1:T(8,128)}, ...), branch_computations={%region_20.21_spmd, %region_21.22_spmd.clone} | conditional | flops 675940864 | bytes 15033202 | solution.py:157
  624.9 14.0 %conditional.17 = ((f32[2560,2,128]{0,2,1:T(8,128)}, f32[2560,2,128]{0,2,1:T(8,128)}, f32[2560,2,128]{0,2,1:T(8,128)S(1)})) conditional(s32[]{:T(128)} %bitcast.135, (f32[2560,2,128]{0,2,1:T(8,128)}, f32[2560,2,128]{0,2,1:T(8,128)}, f32[2560,2,128]{0,2,1:T(8,128)S(1)}) %tuple.202, (s32[]{:T(128)}, f32[2560,2,128]{0,2,1:T(8,128)}, ...), branch_computations={%region_20.21_spmd, %region_21.22_spmd.clone} | conditional | flops 675940864 | bytes 15033202 | solution.py:157
  640.2 13.9 %conditional.17 = ((f32[2560,2,128]{0,2,1:T(8,128)}, f32[2560,2,128]{0,2,1:T(8,128)}, f32[2560,2,128]{0,2,1:T(8,128)S(1)})) conditional(s32[]{:T(128)} %bitcast.135, (f32[2560,2,128]{0,2,1:T(8,128)}, f32[2560,2,128]{0,2,1:T(8,128)}, f32[2560,2,128]{0,2,1:T(8,128)S(1)}) %tuple.202, (s32[]{:T(128)}, f32[2560,2,128]{0,2,1:T(8,128)}, ...), branch_computations={%region_20.21_spmd, %region_21.22_spmd.clone} | conditional | flops 675940864 | bytes 15033202 | solution.py:157
  655.4 14.0 %conditional.17 = ((f32[2560,2,128]{0,2,1:T(8,128)}, f32[2560,2,128]{0,2,1:T(8,128)}, f32[2560,2,128]{0,2,1:T(8,128)S(1)})) conditional(s32[]{:T(128)} %bitcast.135, (f32[2560,2,128]{0,2,1:T(8,128)}, f32[2560,2,128]{0,2,1:T(8,128)}, f32[2560,2,128]{0,2,1:T(8,128)S(1)}) %tuple.202, (s32[]{:T(128)}, f32[2560,2,128]{0,2,1:T(8,128)}, ...), branch_computations={%region_20.21_spmd, %region_21.22_spmd.clone} | conditional | flops 675940864 | bytes 15033202 | solution.py:157
  670.6 14.0 %conditional.17 = ((f32[2560,2,128]{0,2,1:T(8,128)}, f32[2560,2,128]{0,2,1:T(8,128)}, f32[2560,2,128]{0,2,1:T(8,128)S(1)})) conditional(s32[]{:T(128)} %bitcast.135, (f32[2560,2,128]{0,2,1:T(8,128)}, f32[2560,2,128]{0,2,1:T(8,128)}, f32[2560,2,128]{0,2,1:T(8,128)S(1)}) %tuple.202, (s32[]{:T(128)}, f32[2560,2,128]{0,2,1:T(8,128)}, ...), branch_computations={%region_20.21_spmd, %region_21.22_spmd.clone} | conditional | flops 675940864 | bytes 15033202 | solution.py:157
  686.0 14.0 %conditional.17 = ((f32[2560,2,128]{0,2,1:T(8,128)}, f32[2560,2,128]{0,2,1:T(8,128)}, f32[2560,2,128]{0,2,1:T(8,128)S(1)})) conditional(s32[]{:T(128)} %bitcast.135, (f32[2560,2,128]{0,2,1:T(8,128)}, f32[2560,2,128]{0,2,1:T(8,128)}, f32[2560,2,128]{0,2,1:T(8,128)S(1)}) %tuple.202, (s32[]{:T(128)}, f32[2560,2,128]{0,2,1:T(8,128)}, ...), branch_computations={%region_20.21_spmd, %region_21.22_spmd.clone} | conditional | flops 675940864 | bytes 15033202 | solution.py:157
  701.2 14.0 %conditional.17 = ((f32[2560,2,128]{0,2,1:T(8,128)}, f32[2560,2,128]{0,2,1:T(8,128)}, f32[2560,2,128]{0,2,1:T(8,128)S(1)})) conditional(s32[]{:T(128)} %bitcast.135, (f32[2560,2,128]{0,2,1:T(8,128)}, f32[2560,2,128]{0,2,1:T(8,128)}, f32[2560,2,128]{0,2,1:T(8,128)S(1)}) %tuple.202, (s32[]{:T(128)}, f32[2560,2,128]{0,2,1:T(8,128)}, ...), branch_computations={%region_20.21_spmd, %region_21.22_spmd.clone} | conditional | flops 675940864 | bytes 15033202 | solution.py:157
  716.5 14.0 %conditional.17 = ((f32[2560,2,128]{0,2,1:T(8,128)}, f32[2560,2,128]{0,2,1:T(8,128)}, f32[2560,2,128]{0,2,1:T(8,128)S(1)})) conditional(s32[]{:T(128)} %bitcast.135, (f32[2560,2,128]{0,2,1:T(8,128)}, f32[2560,2,128]{0,2,1:T(8,128)}, f32[2560,2,128]{0,2,1:T(8,128)S(1)}) %tuple.202, (s32[]{:T(128)}, f32[2560,2,128]{0,2,1:T(8,128)}, ...), branch_computations={%region_20.21_spmd, %region_21.22_spmd.clone} | conditional | flops 675940864 | bytes 15033202 | solution.py:157
  731.8 14.1 %conditional.17 = ((f32[2560,2,128]{0,2,1:T(8,128)}, f32[2560,2,128]{0,2,1:T(8,128)}, f32[2560,2,128]{0,2,1:T(8,128)S(1)})) conditional(s32[]{:T(128)} %bitcast.135, (f32[2560,2,128]{0,2,1:T(8,128)}, f32[2560,2,128]{0,2,1:T(8,128)}, f32[2560,2,128]{0,2,1:T(8,128)S(1)}) %tuple.202, (s32[]{:T(128)}, f32[2560,2,128]{0,2,1:T(8,128)}, ...), branch_computations={%region_20.21_spmd, %region_21.22_spmd.clone} | conditional | flops 675940864 | bytes 15033202 | solution.py:157
  747.1 14.0 %conditional.17 = ((f32[2560,2,128]{0,2,1:T(8,128)}, f32[2560,2,128]{0,2,1:T(8,128)}, f32[2560,2,128]{0,2,1:T(8,128)S(1)})) conditional(s32[]{:T(128)} %bitcast.135, (f32[2560,2,128]{0,2,1:T(8,128)}, f32[2560,2,128]{0,2,1:T(8,128)}, f32[2560,2,128]{0,2,1:T(8,128)S(1)}) %tuple.202, (s32[]{:T(128)}, f32[2560,2,128]{0,2,1:T(8,128)}, ...), branch_computations={%region_20.21_spmd, %region_21.22_spmd.clone} | conditional | flops 675940864 | bytes 15033202 | solution.py:157
  781.2 10.1 all-to-all-done.8
  799.9 11.6 %all-to-all-done.10 = bf16[160,16,1,2,128]{4,0,3,2,1:T(8,128)(2,1)} async-done(((bf16[160,16,1,2,128]{4,0,3,2,1:T(8,128)(2,1)}), bf16[160,16,1,2,128]{4,0,3,2,1:T(8,128)(2,1)}, u32[]{:S(2)}, u32[]{:S(2)}) %all-to-all-start.10) | async-done | bytes 1310752 | tf_op jit(solution)/shard_map/all_to_all | solution.py:192
  817.7 13.2 %all-to-all-done.12 = bf16[160,16,1,2,128]{4,0,3,2,1:T(8,128)(2,1)S(1)} async-done(((bf16[160,16,1,2,128]{4,0,3,2,1:T(8,128)(2,1)}), bf16[160,16,1,2,128]{4,0,3,2,1:T(8,128)(2,1)S(1)}, u32[]{:S(2)}, u32[]{:S(2)}) %all-to-all-start.12) | async-done | bytes 1310752 | tf_op jit(solution)/shard_map/all_to_all | solution.py:193
  850.5 12.8 %all-to-all-start.9 = ((bf16[10,16,4096]{2,0,1:T(8,128)(2,1)}), bf16[10,16,4096]{2,0,1:T(8,128)(2,1)S(1)}, u32[]{:S(2)}, u32[]{:S(2)}) async-start(bf16[10,16,4096]{2,0,1:T(8,128)(2,1)} %copy.177), calls=%async_computation.9 | async-start | bytes 4194304 | tf_op jit(solution)/shard_map/all_to_all | solution.py:199
  874.4 37.7 %all-to-all-done.9 = bf16[10,16,4096]{2,0,1:T(8,128)(2,1)S(1)} async-done(((bf16[10,16,4096]{2,0,1:T(8,128)(2,1)}), bf16[10,16,4096]{2,0,1:T(8,128)(2,1)S(1)}, u32[]{:S(2)}, u32[]{:S(2)}) %all-to-all-start.9) | async-done | bytes 1310752 | tf_op jit(solution)/shard_map/all_to_all | solution.py:199
  928.2 37.9 %all-to-all-done.11 = bf16[10,16,4096]{2,0,1:T(8,128)(2,1)} async-done(((bf16[10,16,4096]{2,0,1:T(8,128)(2,1)}), bf16[10,16,4096]{2,0,1:T(8,128)(2,1)}, u32[]{:S(2)}, u32[]{:S(2)}) %all-to-all-start.11) | async-done | bytes 1310752 | tf_op jit(solution)/shard_map/all_to_all | solution.py:200
  983.4 37.0 %all-to-all-done.13 = bf16[10,16,4096]{2,0,1:T(8,128)(2,1)} async-done(((bf16[10,16,4096]{2,0,1:T(8,128)(2,1)}), bf16[10,16,4096]{2,0,1:T(8,128)(2,1)}, u32[]{:S(2)}, u32[]{:S(2)}) %all-to-all-start.13) | async-done | bytes 1310752 | tf_op jit(solution)/shard_map/all_to_all | solution.py:201
  (832 shorter events, 795.4 us)
Async XLA Ops:
  0.6 13.5 %copy-start = (bf16[128,1,4096]{2,0,1:T(8,128)(2,1)S(1)}, bf16[128,1,4096]{2,0,1:T(8,128)(2,1)}, u32[]{:S(2)}) copy-start(bf16[128,1,4096]{2,0,1:T(8,128)(2,1)} %param.26) | copy-start | bytes 3145732
  5.9 7.7 copy-start.10
  5.9 7.7 copy-start.13
  5.9 30.5 %all-to-all-start.7 = ((bf16[160,1,16,2,128]{4,0,3,1,2:T(8,128)(2,1)}), bf16[160,1,16,2,128]{4,0,3,1,2:T(8,128)(2,1)S(1)}, u32[]{:S(2)}, u32[]{:S(2)}) async-start(bf16[160,1,16,2,128]{4,0,3,1,2:T(8,128)(2,1)} %copy.172), calls=%async_computation.7 | async-start | bytes 2621440 | tf_op jit(solution)/shard_map/all_to_all | solution.py:184
  14.2 2.4 copy-start.2
  16.6 2.4 copy-start.3
  150.7 52.1 %all-to-all-start = ((bf16[10,16,4096]{2,0,1:T(8,128)(2,1)}), bf16[10,16,4096]{2,0,1:T(8,128)(2,1)S(1)}, u32[]{:S(2)}, u32[]{:S(2)}) async-start(bf16[10,16,4096]{2,0,1:T(8,128)(2,1)} %get-tuple-element.1228), calls=%async_computation | async-start | bytes 4194304 | tf_op jit(solution)/shard_map/all_to_all | solution.py:175
  202.8 27.4 %all-to-all-start.3 = ((bf16[160,1,16,2,128]{4,0,3,1,2:T(8,128)(2,1)}), bf16[160,1,16,2,128]{4,0,3,1,2:T(8,128)(2,1)}, u32[]{:S(2)}, u32[]{:S(2)}) async-start(bf16[160,1,16,2,128]{4,0,3,1,2:T(8,128)(2,1)} %copy.162), calls=%async_computation.3 | async-start | bytes 2621440 | tf_op jit(solution)/shard_map/all_to_all | solution.py:182
  230.2 22.2 %all-to-all-start.5 = ((bf16[160,1,16,2,128]{4,0,3,1,2:T(8,128)(2,1)}), bf16[160,1,16,2,128]{4,0,3,1,2:T(8,128)(2,1)}, u32[]{:S(2)}, u32[]{:S(2)}) async-start(bf16[160,1,16,2,128]{4,0,3,1,2:T(8,128)(2,1)} %copy.166), calls=%async_computation.5 | async-start | bytes 2621440 | tf_op jit(solution)/shard_map/all_to_all | solution.py:181
  243.5 16.1 %copy-start.12 = (s32[15]{0:T(128)S(1)}, s32[15]{0:T(128)}, u32[]{:S(2)}) copy-start(s32[15]{0:T(128)} %constant.203) | copy-start | bytes 184
  252.5 135.6 %all-to-all-start.1 = ((bf16[160,1,16,2,128]{4,0,3,1,2:T(8,128)(2,1)}), bf16[160,1,16,2,128]{4,0,3,1,2:T(8,128)(2,1)}, u32[]{:S(2)}, u32[]{:S(2)}) async-start(bf16[160,1,16,2,128]{4,0,3,1,2:T(8,128)(2,1)} %copy.158), calls=%async_computation.1 | async-start | bytes 2621440 | tf_op jit(solution)/shard_map/all_to_all | solution.py:183
  257.6 3.5 copy-start.11
  263.5 263.0 %copy-start.4 = (bf16[160,1,16,2,128]{4,2,0,3,1:T(8,128)(2,1)}, bf16[160,1,16,2,128]{4,2,0,3,1:T(8,128)(2,1)S(1)}, u32[]{:S(2)}) copy-start(bf16[160,1,16,2,128]{4,2,0,3,1:T(8,128)(2,1)S(1)} %copy.173) | copy-start | bytes 3932164
  387.0 1.1 copy-start.8
  390.2 3.5 copy-start.5
  526.5 1.1 copy-start.6
  767.8 23.5 %all-to-all-start.8 = ((bf16[160,16,1,2,128]{4,0,3,2,1:T(8,128)(2,1)}), bf16[160,16,1,2,128]{4,0,3,2,1:T(8,128)(2,1)}, u32[]{:S(2)}, u32[]{:S(2)}) async-start(bf16[160,16,1,2,128]{4,0,3,2,1:T(8,128)(2,1)} %copy.175), calls=%async_computation.8 | async-start | bytes 2621440 | tf_op jit(solution)/shard_map/all_to_all | solution.py:191
  791.3 20.2 %all-to-all-start.10 = ((bf16[160,16,1,2,128]{4,0,3,2,1:T(8,128)(2,1)}), bf16[160,16,1,2,128]{4,0,3,2,1:T(8,128)(2,1)}, u32[]{:S(2)}, u32[]{:S(2)}) async-start(bf16[160,16,1,2,128]{4,0,3,2,1:T(8,128)(2,1)} %copy.180), calls=%async_computation.10 | async-start | bytes 2621440 | tf_op jit(solution)/shard_map/all_to_all | solution.py:192
  799.9 15.3 %copy-start.7 = (bf16[2560,2,128]{2,0,1:T(8,128)(2,1)S(1)}, bf16[2560,2,128]{2,0,1:T(8,128)(2,1)}, u32[]{:S(2)}) copy-start(bf16[2560,2,128]{2,0,1:T(8,128)(2,1)} %copy-done.6) | copy-start | bytes 3932164
  811.5 19.3 %all-to-all-start.12 = ((bf16[160,16,1,2,128]{4,0,3,2,1:T(8,128)(2,1)}), bf16[160,16,1,2,128]{4,0,3,2,1:T(8,128)(2,1)S(1)}, u32[]{:S(2)}, u32[]{:S(2)}) async-start(bf16[160,16,1,2,128]{4,0,3,2,1:T(8,128)(2,1)} %copy.185), calls=%async_computation.12 | async-start | bytes 2621440 | tf_op jit(solution)/shard_map/all_to_all | solution.py:193
  830.8 1.1 copy-start.9
  831.9 18.6 %all-to-all-start.6 = ((bf16[160,16,1,2,128]{4,3,0,2,1:T(2,128)(2,1)}), bf16[160,16,1,2,128]{4,3,0,2,1:T(2,128)(2,1)S(1)}, u32[]{:S(2)}, u32[]{:S(2)}) async-start(bf16[160,16,1,2,128]{4,3,0,2,1:T(2,128)(2,1)} %copy.170), calls=%async_computation.6 | async-start | bytes 2621440 | tf_op jit(solution)/shard_map/all_to_all | solution.py:190
  850.5 61.7 %all-to-all-start.9 = ((bf16[10,16,4096]{2,0,1:T(8,128)(2,1)}), bf16[10,16,4096]{2,0,1:T(8,128)(2,1)S(1)}, u32[]{:S(2)}, u32[]{:S(2)}) async-start(bf16[10,16,4096]{2,0,1:T(8,128)(2,1)} %copy.177), calls=%async_computation.9 | async-start | bytes 4194304 | tf_op jit(solution)/shard_map/all_to_all | solution.py:199
  912.1 54.0 %all-to-all-start.11 = ((bf16[10,16,4096]{2,0,1:T(8,128)(2,1)}), bf16[10,16,4096]{2,0,1:T(8,128)(2,1)}, u32[]{:S(2)}, u32[]{:S(2)}) async-start(bf16[10,16,4096]{2,0,1:T(8,128)(2,1)} %copy.182), calls=%async_computation.11 | async-start | bytes 4194304 | tf_op jit(solution)/shard_map/all_to_all | solution.py:200
  966.2 54.2 %all-to-all-start.13 = ((bf16[10,16,4096]{2,0,1:T(8,128)(2,1)}), bf16[10,16,4096]{2,0,1:T(8,128)(2,1)}, u32[]{:S(2)}, u32[]{:S(2)}) async-start(bf16[10,16,4096]{2,0,1:T(8,128)(2,1)} %copy.187), calls=%async_computation.13 | async-start | bytes 4194304 | tf_op jit(solution)/shard_map/all_to_all | solution.py:201
  1024.9 3.1 copy-start.1
where the time goes:
time: 1040 us; the launch traced here: 1030 us
  local copies, waits for them, and re-layouts  283 us (27%)
  waiting for transfers between devices  211 us (20%)
  matrix products  210 us (20%)
  blocking collectives  114 us (11%)
  loops' own time  92.3 us (9%)
  starting transfers between devices  69.7 us (7%)
  other arithmetic  46.9 us (5%)
    all_to_all x1, blocking collectives, to_groups(): lax.all_to_all(second_part, 'dp', split_axis=1, concat_axis=1, tiled=True)  60.6 us
    dynamic_slice x45, local copies, waits for them, and re-layouts, tile_scores(): q_start = query_block[pair_index] * block_rows  56.3 us
    dynamic_slice x45, local copies, waits for them, and re-layouts, tile_scores(): k_start = key_block[pair_index] * block_rows  56.3 us
    all_to_all x1, blocking collectives, to_groups(): lax.all_to_all(first_part, 'dp', split_axis=1, concat_axis=1, tiled=True)  53.7 us
    dot_general x30, matrix products, tile_scores(): jnp.einsum('qhe,khe->qhk', q_rows, k_rows, preferred_element_type=jnp.flo...  49.3 us
    dot_general x15, matrix products, value_compute(): jnp.einsum('qhk,khe->qhe', weight, v_rows, preferred_element_type=jnp.flo...  44.9 us
    all_to_all x1, waiting for transfers between devices, to_packed(): lax.all_to_all(second_part, 'dp', split_axis=1, concat_axis=1, tiled=True)  37.9 us
    all_to_all x1, waiting for transfers between devices, to_packed(): lax.all_to_all(first_part, 'dp', split_axis=1, concat_axis=1, tiled=True)  37.7 us
  transfers between devices with their start and end apart: 12, of which 10 were waited for; matrix products, arithmetic and copies ran while one was open for 20% of the time, Pallas kernels for 0%

commit v1 on v0

--- a/solution.py
+++ b/solution.py
@@ -198,7 +198,12 @@
     return (
         lax.all_to_all(first_part, "dp", split_axis=1, concat_axis=1, tiled=True),
         lax.all_to_all(second_part, "dp", split_axis=1, concat_axis=1, tiled=True),
-        lax.all_to_all(third_part, "dp", split_axis=1, concat_axis=1, tiled=True),
+        jnp.concatenate(
+            lax.all_to_all(
+                jnp.stack(jnp.split(third_part, lax.axis_size("dp"), axis=1)), "dp", 0, 0
+            ),
+            axis=1,
+        ),
     )
 
 

time: 1040 us -> 1040 us (level)
    unnamed x29 -> x54, local copies, waits for them, and re-layouts: 4.04 us -> 14.8 us
    all_to_all x1, waiting for transfers between devices: 13.2 us -> 2.43 us  [from_heads(): lax.all_to_all(fourth_part, 'seq', split_axis=1, concat_axis=2, tiled=True)]
  transfers between devices with their start and end apart: 12 -> 12, of which waited for: 10 -> 9; matrix products, arithmetic and copies ran while one was open for 20% -> 20% of each run, Pallas kernels for 0% -> 0%
where the time goes in v1:
time: 1040 us; the launch traced here: 1030 us
  local copies, waits for them, and re-layouts  283 us (27%)
  matrix products  211 us (20%)
  waiting for transfers between devices  210 us (20%)
  blocking collectives  114 us (11%)
  loops' own time  88.7 us (9%)
  starting transfers between devices  72.4 us (7%)
  other arithmetic  46.9 us (5%)
    all_to_all x1, blocking collectives, to_groups(): lax.all_to_all(second_part, 'dp', split_axis=1, concat_axis=1, tiled=True)  60.6 us
    dynamic_slice x45, local copies, waits for them, and re-layouts, tile_scores(): q_start = query_block[pair_index] * block_rows  55.9 us
    dynamic_slice x45, local copies, waits for them, and re-layouts, tile_scores(): k_start = key_block[pair_index] * block_rows  55.9 us
    all_to_all x1, blocking collectives, to_groups(): lax.all_to_all(first_part, 'dp', split_axis=1, concat_axis=1, tiled=True)  53.7 us
    dot_general x30, matrix products, tile_scores(): jnp.einsum('qhe,khe->qhk', q_rows, k_rows, preferred_element_type=jnp.flo...  49.3 us
    dot_general x15, matrix products, value_compute(): jnp.einsum('qhk,khe->qhe', weight, v_rows, preferred_element_type=jnp.flo...  45.1 us
    all_to_all x1, waiting for transfers between devices, to_packed(): lax.all_to_all(jnp.stack(jnp.split(third_part, lax.axis_size('dp'), axis=...  41.4 us
    all_to_all x1, waiting for transfers between devices, to_packed(): lax.all_to_all(first_part, 'dp', split_axis=1, concat_axis=1, tiled=True)  41.3 us
  transfers between devices with their start and end apart: 12, of which 9 were waited for; matrix products, arithmetic and copies ran while one was open for 20% of the time, Pallas kernels for 0%

profile of v1, /device:TPU:1, one launch (start us, length us, event | category | flops | bytes accessed | tf_op | source)
XLA Modules:
  0.0 1027.9 jit_solution(17507517473948000731)
XLA Ops:
  5.9 7.6 all-to-all-start.7
  25.8 10.6 %copy_select_fusion = (bf16[10,16,4096]{2,0,1:T(8,128)(2,1)S(1)}, bf16[10,16,4096]{2,0,1:T(8,128)(2,1)}, bf16[10,16,4096]{2,0,1:T(8,128)(2,1)}) fusion(bf16[10,16,4096]{2,1,0:T(8,128)(2,1)} %bitcast.186, pred[10,16]{0,1:T(8,128)(4,1)S(1)} %copy.597, bf16[10,16,4096]{2,1,0:T(8,128)(2,1)} %bitcast.187, bf16[10,16,4096]{2,1,0:T(8,128)(2,1)} %bitcast.188), kind=kLoop, calls=%fused_computation.84 | loop fusion | flops 1966080 | bytes 7864480 | tf_op jit(solution)/shard_map/jit(_where)/select_n | solution.py:240
  36.3 60.6 %all_to_all.102 = bf16[10,16,4096]{2,0,1:T(8,128)(2,1)} all-to-all(bf16[10,16,4096]{2,0,1:T(8,128)(2,1)} %get-tuple-element.1383), channel_id=1, replica_groups=mesh['seq'=16,'dp'=16] {'dp'}, dimensions={1} | all-to-all | bytes 2621440 | tf_op jit(solution)/shard_map/all_to_all | solution.py:174
  96.9 53.7 %all_to_all.103 = bf16[10,16,4096]{2,0,1:T(8,128)(2,1)} all-to-all(bf16[10,16,4096]{2,0,1:T(8,128)(2,1)S(1)} %get-tuple-element.1382), channel_id=1, replica_groups=mesh['seq'=16,'dp'=16] {'dp'}, dimensions={1} | all-to-all | bytes 2621440 | tf_op jit(solution)/shard_map/all_to_all | solution.py:173
  165.1 37.7 %all-to-all-done = bf16[10,16,4096]{2,0,1:T(8,128)(2,1)S(1)} async-done(((bf16[10,16,4096]{2,0,1:T(8,128)(2,1)}), bf16[10,16,4096]{2,0,1:T(8,128)(2,1)S(1)}, u32[]{:S(2)}, u32[]{:S(2)}) %all-to-all-start) | async-done | bytes 1310752 | tf_op jit(solution)/shard_map/all_to_all | solution.py:175
  220.4 9.8 all-to-all-done.3
  242.8 9.7 all-to-all-done.5
  270.2 113.0 %while.54 = (s32[]{:T(128)}, f32[2560,2]{0,1:T(2,128)S(1)}, f32[2560,2]{0,1:T(2,128)S(1)}, pred[15]{0:T(512)(128)(4,1)S(1)}, s32[2560]{0:T(1024)S(1)}, /*index=5...) while((s32[]{:T(128)}, f32[2560,2]{0,1:T(2,128)S(1)}, ...), condition=%wide.region_13.15_spmd.clone.clone, body=%wide.region_8.14_spmd.sunk.clone.clone.sunk | while | flops 138678800 | bytes 5712918 | solution.py:85
  389.9 131.0 %while.55 = (s32[]{:T(128)}, f32[2560,2,128]{0,2,1:T(8,128)}, pred[15]{0:T(512)(128)(4,1)S(1)}, bf16[2560,2,128]{0,2,1:T(8,128)(2,1)}, s32[2560]{0:T(1024)S(1)},...) while((s32[]{:T(128)}, f32[2560,2,128]{0,2,1:T(8,128)}, ...), condition=%wide.region_17.19_spmd.clone.clone, body=%wide.region_14.18_spmd.sunk.clone.clone.sunk | while | flops 271452672 | bytes 2450426 | solution.py:105
  478.3 7.5 conditional.16
  527.7 229.7 %while.56 = (s32[]{:T(128)}, f32[2560,2,128]{0,2,1:T(8,128)}, f32[2560,2,128]{0,2,1:T(8,128)}, f32[2560,2,128]{0,2,1:T(8,128)S(1)}, pred[15]{0:T(512)(128)(4,1)S...) while((s32[]{:T(128)}, f32[2560,2,128]{0,2,1:T(8,128)}, ...), condition=%wide.region_22.24_spmd.clone.clone, body=%wide.region_19.23_spmd.sunk.clone.clone.sunk | while | flops 675940864 | bytes 15043730 | solution.py:160
  529.2 14.0 %conditional.17 = ((f32[2560,2,128]{0,2,1:T(8,128)}, f32[2560,2,128]{0,2,1:T(8,128)}, f32[2560,2,128]{0,2,1:T(8,128)S(1)})) conditional(s32[]{:T(128)} %bitcast.168, (f32[2560,2,128]{0,2,1:T(8,128)}, f32[2560,2,128]{0,2,1:T(8,128)}, f32[2560,2,128]{0,2,1:T(8,128)S(1)}) %tuple.232, (s32[]{:T(128)}, f32[2560,2,128]{0,2,1:T(8,128)}, ...), branch_computations={%region_20.21_spmd, %region_21.22_spmd.clone} | conditional | flops 675940864 | bytes 15033202 | solution.py:157
  544.5 14.0 %conditional.17 = ((f32[2560,2,128]{0,2,1:T(8,128)}, f32[2560,2,128]{0,2,1:T(8,128)}, f32[2560,2,128]{0,2,1:T(8,128)S(1)})) conditional(s32[]{:T(128)} %bitcast.168, (f32[2560,2,128]{0,2,1:T(8,128)}, f32[2560,2,128]{0,2,1:T(8,128)}, f32[2560,2,128]{0,2,1:T(8,128)S(1)}) %tuple.232, (s32[]{:T(128)}, f32[2560,2,128]{0,2,1:T(8,128)}, ...), branch_computations={%region_20.21_spmd, %region_21.22_spmd.clone} | conditional | flops 675940864 | bytes 15033202 | solution.py:157
  559.7 14.0 %conditional.17 = ((f32[2560,2,128]{0,2,1:T(8,128)}, f32[2560,2,128]{0,2,1:T(8,128)}, f32[2560,2,128]{0,2,1:T(8,128)S(1)})) conditional(s32[]{:T(128)} %bitcast.168, (f32[2560,2,128]{0,2,1:T(8,128)}, f32[2560,2,128]{0,2,1:T(8,128)}, f32[2560,2,128]{0,2,1:T(8,128)S(1)}) %tuple.232, (s32[]{:T(128)}, f32[2560,2,128]{0,2,1:T(8,128)}, ...), branch_computations={%region_20.21_spmd, %region_21.22_spmd.clone} | conditional | flops 675940864 | bytes 15033202 | solution.py:157
  575.0 14.0 %conditional.17 = ((f32[2560,2,128]{0,2,1:T(8,128)}, f32[2560,2,128]{0,2,1:T(8,128)}, f32[2560,2,128]{0,2,1:T(8,128)S(1)})) conditional(s32[]{:T(128)} %bitcast.168, (f32[2560,2,128]{0,2,1:T(8,128)}, f32[2560,2,128]{0,2,1:T(8,128)}, f32[2560,2,128]{0,2,1:T(8,128)S(1)}) %tuple.232, (s32[]{:T(128)}, f32[2560,2,128]{0,2,1:T(8,128)}, ...), branch_computations={%region_20.21_spmd, %region_21.22_spmd.clone} | conditional | flops 675940864 | bytes 15033202 | solution.py:157
  590.3 14.1 %conditional.17 = ((f32[2560,2,128]{0,2,1:T(8,128)}, f32[2560,2,128]{0,2,1:T(8,128)}, f32[2560,2,128]{0,2,1:T(8,128)S(1)})) conditional(s32[]{:T(128)} %bitcast.168, (f32[2560,2,128]{0,2,1:T(8,128)}, f32[2560,2,128]{0,2,1:T(8,128)}, f32[2560,2,128]{0,2,1:T(8,128)S(1)}) %tuple.232, (s32[]{:T(128)}, f32[2560,2,128]{0,2,1:T(8,128)}, ...), branch_computations={%region_20.21_spmd, %region_21.22_spmd.clone} | conditional | flops 675940864 | bytes 15033202 | solution.py:157
  605.6 14.0 %conditional.17 = ((f32[2560,2,128]{0,2,1:T(8,128)}, f32[2560,2,128]{0,2,1:T(8,128)}, f32[2560,2,128]{0,2,1:T(8,128)S(1)})) conditional(s32[]{:T(128)} %bitcast.168, (f32[2560,2,128]{0,2,1:T(8,128)}, f32[2560,2,128]{0,2,1:T(8,128)}, f32[2560,2,128]{0,2,1:T(8,128)S(1)}) %tuple.232, (s32[]{:T(128)}, f32[2560,2,128]{0,2,1:T(8,128)}, ...), branch_computations={%region_20.21_spmd, %region_21.22_spmd.clone} | conditional | flops 675940864 | bytes 15033202 | solution.py:157
  620.9 14.0 %conditional.17 = ((f32[2560,2,128]{0,2,1:T(8,128)}, f32[2560,2,128]{0,2,1:T(8,128)}, f32[2560,2,128]{0,2,1:T(8,128)S(1)})) conditional(s32[]{:T(128)} %bitcast.168, (f32[2560,2,128]{0,2,1:T(8,128)}, f32[2560,2,128]{0,2,1:T(8,128)}, f32[2560,2,128]{0,2,1:T(8,128)S(1)}) %tuple.232, (s32[]{:T(128)}, f32[2560,2,128]{0,2,1:T(8,128)}, ...), branch_computations={%region_20.21_spmd, %region_21.22_spmd.clone} | conditional | flops 675940864 | bytes 15033202 | solution.py:157
  636.2 14.0 %conditional.17 = ((f32[2560,2,128]{0,2,1:T(8,128)}, f32[2560,2,128]{0,2,1:T(8,128)}, f32[2560,2,128]{0,2,1:T(8,128)S(1)})) conditional(s32[]{:T(128)} %bitcast.168, (f32[2560,2,128]{0,2,1:T(8,128)}, f32[2560,2,128]{0,2,1:T(8,128)}, f32[2560,2,128]{0,2,1:T(8,128)S(1)}) %tuple.232, (s32[]{:T(128)}, f32[2560,2,128]{0,2,1:T(8,128)}, ...), branch_computations={%region_20.21_spmd, %region_21.22_spmd.clone} | conditional | flops 675940864 | bytes 15033202 | solution.py:157
  651.5 14.0 %conditional.17 = ((f32[2560,2,128]{0,2,1:T(8,128)}, f32[2560,2,128]{0,2,1:T(8,128)}, f32[2560,2,128]{0,2,1:T(8,128)S(1)})) conditional(s32[]{:T(128)} %bitcast.168, (f32[2560,2,128]{0,2,1:T(8,128)}, f32[2560,2,128]{0,2,1:T(8,128)}, f32[2560,2,128]{0,2,1:T(8,128)S(1)}) %tuple.232, (s32[]{:T(128)}, f32[2560,2,128]{0,2,1:T(8,128)}, ...), branch_computations={%region_20.21_spmd, %region_21.22_spmd.clone} | conditional | flops 675940864 | bytes 15033202 | solution.py:157
  666.8 14.0 %conditional.17 = ((f32[2560,2,128]{0,2,1:T(8,128)}, f32[2560,2,128]{0,2,1:T(8,128)}, f32[2560,2,128]{0,2,1:T(8,128)S(1)})) conditional(s32[]{:T(128)} %bitcast.168, (f32[2560,2,128]{0,2,1:T(8,128)}, f32[2560,2,128]{0,2,1:T(8,128)}, f32[2560,2,128]{0,2,1:T(8,128)S(1)}) %tuple.232, (s32[]{:T(128)}, f32[2560,2,128]{0,2,1:T(8,128)}, ...), branch_computations={%region_20.21_spmd, %region_21.22_spmd.clone} | conditional | flops 675940864 | bytes 15033202 | solution.py:157
  682.0 14.0 %conditional.17 = ((f32[2560,2,128]{0,2,1:T(8,128)}, f32[2560,2,128]{0,2,1:T(8,128)}, f32[2560,2,128]{0,2,1:T(8,128)S(1)})) conditional(s32[]{:T(128)} %bitcast.168, (f32[2560,2,128]{0,2,1:T(8,128)}, f32[2560,2,128]{0,2,1:T(8,128)}, f32[2560,2,128]{0,2,1:T(8,128)S(1)}) %tuple.232, (s32[]{:T(128)}, f32[2560,2,128]{0,2,1:T(8,128)}, ...), branch_computations={%region_20.21_spmd, %region_21.22_spmd.clone} | conditional | flops 675940864 | bytes 15033202 | solution.py:157
  697.4 14.1 %conditional.17 = ((f32[2560,2,128]{0,2,1:T(8,128)}, f32[2560,2,128]{0,2,1:T(8,128)}, f32[2560,2,128]{0,2,1:T(8,128)S(1)})) conditional(s32[]{:T(128)} %bitcast.168, (f32[2560,2,128]{0,2,1:T(8,128)}, f32[2560,2,128]{0,2,1:T(8,128)}, f32[2560,2,128]{0,2,1:T(8,128)S(1)}) %tuple.232, (s32[]{:T(128)}, f32[2560,2,128]{0,2,1:T(8,128)}, ...), branch_computations={%region_20.21_spmd, %region_21.22_spmd.clone} | conditional | flops 675940864 | bytes 15033202 | solution.py:157
  712.7 14.1 %conditional.17 = ((f32[2560,2,128]{0,2,1:T(8,128)}, f32[2560,2,128]{0,2,1:T(8,128)}, f32[2560,2,128]{0,2,1:T(8,128)S(1)})) conditional(s32[]{:T(128)} %bitcast.168, (f32[2560,2,128]{0,2,1:T(8,128)}, f32[2560,2,128]{0,2,1:T(8,128)}, f32[2560,2,128]{0,2,1:T(8,128)S(1)}) %tuple.232, (s32[]{:T(128)}, f32[2560,2,128]{0,2,1:T(8,128)}, ...), branch_computations={%region_20.21_spmd, %region_21.22_spmd.clone} | conditional | flops 675940864 | bytes 15033202 | solution.py:157
  728.1 14.0 %conditional.17 = ((f32[2560,2,128]{0,2,1:T(8,128)}, f32[2560,2,128]{0,2,1:T(8,128)}, f32[2560,2,128]{0,2,1:T(8,128)S(1)})) conditional(s32[]{:T(128)} %bitcast.168, (f32[2560,2,128]{0,2,1:T(8,128)}, f32[2560,2,128]{0,2,1:T(8,128)}, f32[2560,2,128]{0,2,1:T(8,128)S(1)}) %tuple.232, (s32[]{:T(128)}, f32[2560,2,128]{0,2,1:T(8,128)}, ...), branch_computations={%region_20.21_spmd, %region_21.22_spmd.clone} | conditional | flops 675940864 | bytes 15033202 | solution.py:157
  743.4 14.0 %conditional.17 = ((f32[2560,2,128]{0,2,1:T(8,128)}, f32[2560,2,128]{0,2,1:T(8,128)}, f32[2560,2,128]{0,2,1:T(8,128)S(1)})) conditional(s32[]{:T(128)} %bitcast.168, (f32[2560,2,128]{0,2,1:T(8,128)}, f32[2560,2,128]{0,2,1:T(8,128)}, f32[2560,2,128]{0,2,1:T(8,128)S(1)}) %tuple.232, (s32[]{:T(128)}, f32[2560,2,128]{0,2,1:T(8,128)}, ...), branch_computations={%region_20.21_spmd, %region_21.22_spmd.clone} | conditional | flops 675940864 | bytes 15033202 | solution.py:157
  816.6 14.3 %all-to-all-done.10 = bf16[160,16,1,2,128]{4,0,3,2,1:T(8,128)(2,1)S(1)} async-done(((bf16[160,16,1,2,128]{4,0,3,2,1:T(8,128)(2,1)}), bf16[160,16,1,2,128]{4,0,3,2,1:T(8,128)(2,1)S(1)}, u32[]{:S(2)}, u32[]{:S(2)}) %all-to-all-start.10) | async-done | bytes 1310752 | tf_op jit(solution)/shard_map/all_to_all | solution.py:192
  836.8 14.1 %all-to-all-done.6 = bf16[160,16,1,2,128]{4,3,0,2,1:T(2,128)(2,1)} async-done(((bf16[160,16,1,2,128]{4,3,0,2,1:T(2,128)(2,1)}), bf16[160,16,1,2,128]{4,3,0,2,1:T(2,128)(2,1)}, u32[]{:S(2)}, u32[]{:S(2)}) %all-to-all-start.6) | async-done | bytes 1310752 | tf_op jit(solution)/shard_map/all_to_all | solution.py:190
  851.0 11.6 %all-to-all-start.13 = ((bf16[16,10,1,4096]{3,1,2,0:T(8,128)(2,1)}), bf16[16,10,1,4096]{3,1,2,0:T(8,128)(2,1)S(1)}, u32[]{:S(2)}, u32[]{:S(2)}) async-start(bf16[16,10,1,4096]{3,1,2,0:T(8,128)(2,1)} %bitcast_dynamic-update-slice_fusion), calls=%async_computation.13 | async-start | bytes 4194304 | tf_op jit(solution)/shard_map/all_to_all | solution.py:202
  870.2 41.4 %all-to-all-done.13 = bf16[16,10,1,4096]{3,1,2,0:T(8,128)(2,1)S(1)} async-done(((bf16[16,10,1,4096]{3,1,2,0:T(8,128)(2,1)}), bf16[16,10,1,4096]{3,1,2,0:T(8,128)(2,1)S(1)}, u32[]{:S(2)}, u32[]{:S(2)}) %all-to-all-start.13) | async-done | bytes 1310752 | tf_op jit(solution)/shard_map/all_to_all | solution.py:202
  924.5 41.3 %all-to-all-done.9 = bf16[10,16,4096]{2,0,1:T(8,128)(2,1)} async-done(((bf16[10,16,4096]{2,0,1:T(8,128)(2,1)}), bf16[10,16,4096]{2,0,1:T(8,128)(2,1)}, u32[]{:S(2)}, u32[]{:S(2)}) %all-to-all-start.9) | async-done | bytes 1310752 | tf_op jit(solution)/shard_map/all_to_all | solution.py:199
  980.5 39.4 %all-to-all-done.11 = bf16[10,16,4096]{2,0,1:T(8,128)(2,1)} async-done(((bf16[10,16,4096]{2,0,1:T(8,128)(2,1)}), bf16[10,16,4096]{2,0,1:T(8,128)(2,1)}, u32[]{:S(2)}, u32[]{:S(2)}) %all-to-all-start.11) | async-done | bytes 1310752 | tf_op jit(solution)/shard_map/all_to_all | solution.py:200
  (857 shorter events, 785.8 us)
Async XLA Ops:
  0.6 13.4 %copy-start = (bf16[128,1,4096]{2,0,1:T(8,128)(2,1)S(1)}, bf16[128,1,4096]{2,0,1:T(8,128)(2,1)}, u32[]{:S(2)}) copy-start(bf16[128,1,4096]{2,0,1:T(8,128)(2,1)} %param.26) | copy-start | bytes 3145732
  4.3 9.2 copy-start.15
  4.3 9.2 copy-start.18
  4.3 9.7 copy-start.17
  5.9 30.4 %all-to-all-start.7 = ((bf16[160,1,16,2,128]{4,0,3,1,2:T(8,128)(2,1)}), bf16[160,1,16,2,128]{4,0,3,1,2:T(8,128)(2,1)S(1)}, u32[]{:S(2)}, u32[]{:S(2)}) async-start(bf16[160,1,16,2,128]{4,0,3,1,2:T(8,128)(2,1)} %copy.614), calls=%async_computation.7 | async-start | bytes 2621440 | tf_op jit(solution)/shard_map/all_to_all | solution.py:184
  14.1 2.5 copy-start.2
  16.5 2.5 copy-start.3
  150.6 52.1 %all-to-all-start = ((bf16[10,16,4096]{2,0,1:T(8,128)(2,1)}), bf16[10,16,4096]{2,0,1:T(8,128)(2,1)S(1)}, u32[]{:S(2)}, u32[]{:S(2)}) async-start(bf16[10,16,4096]{2,0,1:T(8,128)(2,1)} %get-tuple-element.1384), calls=%async_computation | async-start | bytes 4194304 | tf_op jit(solution)/shard_map/all_to_all | solution.py:175
  202.8 27.4 %all-to-all-start.3 = ((bf16[160,1,16,2,128]{4,0,3,1,2:T(8,128)(2,1)}), bf16[160,1,16,2,128]{4,0,3,1,2:T(8,128)(2,1)}, u32[]{:S(2)}, u32[]{:S(2)}) async-start(bf16[160,1,16,2,128]{4,0,3,1,2:T(8,128)(2,1)} %copy.604), calls=%async_computation.3 | async-start | bytes 2621440 | tf_op jit(solution)/shard_map/all_to_all | solution.py:182
  230.2 22.3 %all-to-all-start.5 = ((bf16[160,1,16,2,128]{4,0,3,1,2:T(8,128)(2,1)}), bf16[160,1,16,2,128]{4,0,3,1,2:T(8,128)(2,1)}, u32[]{:S(2)}, u32[]{:S(2)}) async-start(bf16[160,1,16,2,128]{4,0,3,1,2:T(8,128)(2,1)} %copy.608), calls=%async_computation.5 | async-start | bytes 2621440 | tf_op jit(solution)/shard_map/all_to_all | solution.py:181
  242.8 19.1 %copy-start.16 = (s32[15]{0:T(128)S(1)}, s32[15]{0:T(128)}, u32[]{:S(2)}) copy-start(s32[15]{0:T(128)} %constant.203) | copy-start | bytes 184
  252.5 131.8 %all-to-all-start.1 = ((bf16[160,1,16,2,128]{4,0,3,1,2:T(8,128)(2,1)}), bf16[160,1,16,2,128]{4,0,3,1,2:T(8,128)(2,1)}, u32[]{:S(2)}, u32[]{:S(2)}) async-start(bf16[160,1,16,2,128]{4,0,3,1,2:T(8,128)(2,1)} %copy.600), calls=%async_computation.1 | async-start | bytes 2621440 | tf_op jit(solution)/shard_map/all_to_all | solution.py:183
  264.3 258.7 %copy-start.6 = (bf16[160,1,16,2,128]{4,2,0,3,1:T(8,128)(2,1)}, bf16[160,1,16,2,128]{4,2,0,3,1:T(8,128)(2,1)S(1)}, u32[]{:S(2)}) copy-start(bf16[160,1,16,2,128]{4,2,0,3,1:T(8,128)(2,1)S(1)} %copy.615) | copy-start | bytes 3932164
  383.2 1.1 copy-start.10
  386.4 3.5 copy-start.7
  522.9 2.6 copy-start.8
  759.0 9.8 copy-start.4
  761.9 23.5 %all-to-all-start.12 = ((bf16[160,16,1,2,128]{4,0,3,2,1:T(8,128)(2,1)}), bf16[160,16,1,2,128]{4,0,3,2,1:T(8,128)(2,1)}, u32[]{:S(2)}, u32[]{:S(2)}) async-start(bf16[160,16,1,2,128]{4,0,3,2,1:T(8,128)(2,1)} %copy.627), calls=%async_computation.12 | async-start | bytes 2621440 | tf_op jit(solution)/shard_map/all_to_all | solution.py:193
  772.9 2.2 copy-start.5
  779.2 1.4 copy-start.9
  785.5 22.9 %all-to-all-start.8 = ((bf16[160,16,1,2,128]{4,0,3,2,1:T(8,128)(2,1)}), bf16[160,16,1,2,128]{4,0,3,2,1:T(8,128)(2,1)S(1)}, u32[]{:S(2)}, u32[]{:S(2)}) async-start(bf16[160,16,1,2,128]{4,0,3,2,1:T(8,128)(2,1)} %copy.617), calls=%async_computation.8 | async-start | bytes 2621440 | tf_op jit(solution)/shard_map/all_to_all | solution.py:191
  808.4 22.6 %copy-start.11 = (bf16[160,16,1,2,128]{4,0,3,2,1:T(8,128)(2,1)}, bf16[160,16,1,2,128]{4,0,3,2,1:T(8,128)(2,1)S(1)}, u32[]{:S(2)}) copy-start(bf16[160,16,1,2,128]{4,0,3,2,1:T(8,128)(2,1)S(1)} %all-to-all-done.8) | copy-start | bytes 3932164
  808.4 22.6 %all-to-all-start.10 = ((bf16[160,16,1,2,128]{4,0,3,2,1:T(8,128)(2,1)}), bf16[160,16,1,2,128]{4,0,3,2,1:T(8,128)(2,1)S(1)}, u32[]{:S(2)}, u32[]{:S(2)}) async-start(bf16[160,16,1,2,128]{4,0,3,2,1:T(8,128)(2,1)} %copy.622), calls=%async_computation.10 | async-start | bytes 2621440 | tf_op jit(solution)/shard_map/all_to_all | solution.py:192
  830.9 5.2 copy-start.13
  830.9 20.0 %all-to-all-start.6 = ((bf16[160,16,1,2,128]{4,3,0,2,1:T(2,128)(2,1)}), bf16[160,16,1,2,128]{4,3,0,2,1:T(2,128)(2,1)}, u32[]{:S(2)}, u32[]{:S(2)}) async-start(bf16[160,16,1,2,128]{4,3,0,2,1:T(2,128)(2,1)} %copy.612), calls=%async_computation.6 | async-start | bytes 2621440 | tf_op jit(solution)/shard_map/all_to_all | solution.py:190
  836.8 25.8 %copy-start.12 = (bf16[160,16,1,2,128]{4,0,3,2,1:T(8,128)(2,1)S(1)}, bf16[160,16,1,2,128]{4,0,3,2,1:T(8,128)(2,1)}, u32[]{:S(2)}) copy-start(bf16[160,16,1,2,128]{4,0,3,2,1:T(8,128)(2,1)} %copy-done.11) | copy-start | bytes 3932164
  851.0 60.6 %all-to-all-start.13 = ((bf16[16,10,1,4096]{3,1,2,0:T(8,128)(2,1)}), bf16[16,10,1,4096]{3,1,2,0:T(8,128)(2,1)S(1)}, u32[]{:S(2)}, u32[]{:S(2)}) async-start(bf16[16,10,1,4096]{3,1,2,0:T(8,128)(2,1)} %bitcast_dynamic-update-slice_fusion), calls=%async_computation.13 | async-start | bytes 4194304 | tf_op jit(solution)/shard_map/all_to_all | solution.py:202
  870.2 46.7 %copy-start.14 = (bf16[160,16,1,2,128]{4,0,3,2,1:T(8,128)(2,1)S(1)}, bf16[160,16,1,2,128]{4,0,3,2,1:T(8,128)(2,1)}, u32[]{:S(2)}) copy-start(bf16[160,16,1,2,128]{4,0,3,2,1:T(8,128)(2,1)} %copy-done.13) | copy-start | bytes 3932164
  911.5 54.3 %all-to-all-start.9 = ((bf16[10,16,4096]{2,0,1:T(8,128)(2,1)}), bf16[10,16,4096]{2,0,1:T(8,128)(2,1)}, u32[]{:S(2)}, u32[]{:S(2)}) async-start(bf16[10,16,4096]{2,0,1:T(8,128)(2,1)} %copy.619), calls=%async_computation.9 | async-start | bytes 4194304 | tf_op jit(solution)/shard_map/all_to_all | solution.py:199
  965.8 54.0 %all-to-all-start.11 = ((bf16[10,16,4096]{2,0,1:T(8,128)(2,1)}), bf16[10,16,4096]{2,0,1:T(8,128)(2,1)}, u32[]{:S(2)}, u32[]{:S(2)}) async-start(bf16[10,16,4096]{2,0,1:T(8,128)(2,1)} %copy.624), calls=%async_computation.11 | async-start | bytes 4194304 | tf_op jit(solution)/shard_map/all_to_all | solution.py:200
  1024.3 3.1 copy-start.1
